TPU v7x, 128 devices: a whole 4x4x4 slice. The times are simulated.
128 devices in a mesh: seq: 8 (over z, core), exp: 16 (over x, y).
Axes of the slice: x: 4, y: 4, z: 4, core: 2. Of those that a mesh axis runs over, the one named last changes fastest.
Arguments:
- residual: bfloat16 [16384, 8192], P(('seq', 'exp')), may hold values from -6 to 6
- expert_rows: bfloat16 [8, 16, 16, 24, 8192], P('seq', 'exp'), may hold values from -6 to 6
- expert_ids: int32 [16384, 2], P(('seq', 'exp')), may hold values from 0 to 15, as said below
- expert_slots: int32 [16384, 2], P(('seq', 'exp')), may hold values from 0 to 23, as said below
- combine_weights: float32 [16384, 2], P(('seq', 'exp')), may hold values from 0.1 to 0.9
- norm_gain: float32 [8192], replicated, may hold values from 0.1 to 1.9
- in_weight: bfloat16 [8192, 8192], P(None, 'exp'), may hold values from -0.0625 to 0.0625
- conv_weight: float32 [4, 8192], P(None, 'exp'), may hold values from -3 to 3
- conv_bias: float32 [8192], P('exp'), may hold values from -0.5 to 0.5
- bc_weight: bfloat16 [8192, 128], P('exp'), may hold values from -0.00390625 to 0.00390625
- dt_weight: bfloat16 [8192, 128], P('exp'), may hold values from -0.0625 to 0.0625
- dt_bias: float32 [128], P('exp'), may hold values from -2 to 0.5
- decay_log: float32 [128], P('exp'), may hold values from -14 to -3.2
- skip_gain: float32 [128], P('exp'), may hold values from -1 to 3
Outputs:
- scan_output: bfloat16 [16384, 8192], P('seq', 'exp')
Inputs may be any that keep to these rules, and one draw needn't show every extreme that they name: `expert_ids`: A token's two ids differ. The tokens of one device name no expert more than 24 times, and in each span one expert is named exactly 24 times by the tokens of every device of the span. `expert_slots`: A token's slot at its k-th expert counts the earlier (token, k) pairs of the same device, in row-major order, that name the same expert.
All inputs are finite; a program needn't handle non-finite values.
Results may differ from a plain program's by a relative error of at most 0.0074.
Values may be sent and summed in bfloat16 or wider, within the bound.
No kernel may reach another device: no remote copies, remote signals or barrier semaphores. Data moves between devices by JAX's collectives and lax.ppermute only.
A program may use at most 320 MiB of HBM per device.

v0:
```python
import jax
import jax.numpy as jnp
from jax import lax
from jax.sharding import PartitionSpec as P

TOPK = 2
KCONV = 4
HEAD = 64
NSTATE = 64
STRETCH = 256


def passed_along(value, axis, steps):
    count = lax.axis_size(axis)
    leading, last = (max(0, -steps), min(count, count - steps))
    return lax.ppermute(value, axis, [(source, source + steps) for source in range(leading, last)])


def block_terms(b_rows, c_rows, steps_dt, decays, values):
    running = jnp.cumsum(decays, axis=0)
    scores = jnp.dot(c_rows, b_rows.T, preferred_element_type=jnp.float32)
    length = running.shape[0]
    causal = (jnp.arange(length)[:, None] >= jnp.arange(length)[None, :])[:, :, None]
    decay_gap = jnp.where(causal, running[:, None, :] - running[None, :, :], 0.0)
    mixing = jnp.where(
        causal, jnp.exp(decay_gap) * scores[:, :, None] * steps_dt[None, :, :], 0.0
    ).astype(jnp.bfloat16)
    inside = jnp.einsum("tsh,shp->thp", mixing, values, preferred_element_type=jnp.float32)
    carried = jnp.exp(running[-1][None, :] - running) * steps_dt
    states = jnp.einsum(
        "sn,shp->hnp",
        b_rows.astype(jnp.float32),
        carried[:, :, None] * values.astype(jnp.float32),
        precision=lax.Precision.HIGHEST,
    )
    return (running, inside, states, jnp.exp(running[-1]))


def shards(
    residual,
    expert_rows,
    expert_ids,
    expert_slots,
    combine_weights,
    norm_gain,
    in_weight,
    conv_weight,
    conv_bias,
    bc_weight,
    dt_weight,
    dt_bias,
    decay_log,
    skip_gain,
):
    own_rows, width = residual.shape
    returned = lax.all_to_all(expert_rows, "exp", split_axis=2, concat_axis=1, tiled=True)
    capacity = returned.shape[3]
    buffers = returned.reshape(returned.shape[1] * capacity, width)
    picked = jnp.take(buffers, expert_ids * capacity + expert_slots, axis=0)
    mixture = jnp.zeros((own_rows, width), jnp.float32)
    for column in range(TOPK):
        mixture = mixture + combine_weights[:, column][:, None] * picked[:, column].astype(
            jnp.float32
        )
    stream = residual.astype(jnp.float32) + mixture
    factor = lax.rsqrt(jnp.mean(stream * stream, axis=1, keepdims=True) + 1e-06)
    normed = (stream * factor * norm_gain[None, :]).astype(jnp.bfloat16)
    group_rows = own_rows * lax.axis_size("exp")
    local_width = in_weight.shape[1]
    x_in = jnp.dot(
        lax.all_gather(normed, "exp", axis=0, tiled=True),
        in_weight,
        preferred_element_type=jnp.float32,
    ).astype(jnp.bfloat16)
    rim_rows = passed_along(x_in[group_rows - (KCONV - 1) :], "seq", 1)
    padded = jnp.concatenate([rim_rows, x_in], axis=0)
    filtered = jnp.zeros((group_rows, local_width), jnp.float32) + conv_bias[None, :]
    for tap in range(KCONV):
        filtered = filtered + conv_weight[tap][None, :] * padded[tap : tap + group_rows].astype(
            jnp.float32
        )
    activated = jax.nn.silu(filtered).astype(jnp.bfloat16)
    state_part = jnp.dot(activated, bc_weight, preferred_element_type=jnp.float32)
    rate_part = jnp.dot(activated, dt_weight, preferred_element_type=jnp.float32)
    state_proj, dt_raw = lax.psum((state_part, rate_part), "exp")
    heads_here = local_width // HEAD
    first_head = lax.axis_index("exp") * heads_here
    steps_dt = jax.nn.softplus(
        lax.dynamic_slice_in_dim(dt_raw, first_head, heads_here, 1) + dt_bias[None, :]
    )
    decays = -jnp.exp(decay_log)[None, :] * steps_dt
    b_all = state_proj[:, :NSTATE].astype(jnp.bfloat16)
    c_all = state_proj[:, NSTATE:].astype(jnp.bfloat16)
    blocks = group_rows // STRETCH
    c_blocks = c_all.reshape(blocks, STRETCH, NSTATE)
    value_blocks = activated.reshape(blocks, STRETCH, heads_here, HEAD)

    def advance(carry, inputs):
        local_states, prefix_decay = carry
        b_rows, c_rows, block_dt, block_decays, values = inputs
        running, inside, states, total = block_terms(b_rows, c_rows, block_dt, block_decays, values)
        return (
            (total[:, None, None] * local_states + states, prefix_decay * total),
            (running, inside, local_states, prefix_decay),
        )

    start_carry = (
        jnp.zeros((heads_here, NSTATE, HEAD), jnp.float32),
        jnp.ones((heads_here,), jnp.float32),
    )
    (final_states, device_decay), (runnings, insides, starts, prefixes) = lax.scan(
        advance,
        start_carry,
        (
            b_all.reshape(blocks, STRETCH, NSTATE),
            c_blocks,
            steps_dt.reshape(blocks, STRETCH, heads_here),
            decays.reshape(blocks, STRETCH, heads_here),
            value_blocks,
        ),
    )
    empty_states = jnp.zeros((heads_here, NSTATE, HEAD), jnp.float32)

    def relay_turn(turn, carried):
        incoming, outgoing = carried
        incoming = passed_along(outgoing, "seq", 1)
        return (incoming, device_decay[:, None, None] * incoming + final_states)

    incoming, outgoing_last = lax.fori_loop(
        0, lax.axis_size("seq") - 1, relay_turn, (empty_states, final_states)
    )
    entering = starts + prefixes[:, :, None, None] * incoming[None]
    across = jnp.exp(runnings)[:, :, :, None] * jnp.einsum(
        "btn,bhnp->bthp", c_blocks.astype(jnp.float32), entering, precision=lax.Precision.HIGHEST
    )
    output = insides + across + skip_gain[None, None, :, None] * value_blocks.astype(jnp.float32)
    return output.astype(jnp.bfloat16).reshape(group_rows, local_width)


def solution(mesh):
    placed = (
        P(("seq", "exp"), None),
        P("seq", "exp", None, None, None),
        P(("seq", "exp"), None),
        P(("seq", "exp"), None),
        P(("seq", "exp"), None),
        P(),
        P(None, "exp"),
        P(None, "exp"),
        P("exp"),
        P("exp", None),
        P("exp", None),
        P("exp"),
        P("exp"),
        P("exp"),
    )
    return jax.shard_map(
        shards, mesh=mesh, in_specs=placed, out_specs=P("seq", "exp"), check_vma=False
    )
```

profile of v0, /device:TPU:1, one launch (start us, length us, event | category | flops | bytes accessed | tf_op | source)
XLA Modules:
  0.0 613.9 jit_solution(3130771036729045118)
XLA Ops:
  6.5 7.8 %all-to-all-start = ((bf16[1,1,16,24,8192]{4,3,1,0,2:T(8,128)(2,1)}), bf16[1,1,16,24,8192]{4,3,1,0,2:T(8,128)(2,1)}, u32[]{:S(2)}, u32[]{:S(2)}) async-start(bf16[1,1,16,24,8192]{4,3,1,0,2:T(8,128)(2,1)} %bitcast.113), calls=%async_computation | async-start | bytes 12582912 | tf_op jit(solution)/shard_map/all_to_all | solution.py:56
  14.7 100.4 %all-to-all-done = bf16[1,1,16,24,8192]{4,3,1,0,2:T(8,128)(2,1)} async-done(((bf16[1,1,16,24,8192]{4,3,1,0,2:T(8,128)(2,1)}), bf16[1,1,16,24,8192]{4,3,1,0,2:T(8,128)(2,1)}, u32[]{:S(2)}, u32[]{:S(2)}) %all-to-all-start) | async-done | bytes 6291488 | tf_op jit(solution)/shard_map/all_to_all | solution.py:56
  115.1 12.6 %gather_fusion = bf16[256,8192]{1,0:T(8,128)(2,1)} fusion(bf16[384,8192]{1,0:T(8,128)(2,1)} %bitcast.3, s32[1024]{0:T(1024)S(1)} %pad_clamp_fusion), kind=kCustom, calls=%fused_computation | custom fusion | bytes 8389632 | tf_op jit(solution)/shard_map/jit(_take)/gather | solution.py:59
  127.7 7.6 %reshape.94 = bf16[128,2,8192]{2,1,0:T(2,128)(2,1)} reshape(bf16[256,8192]{1,0:T(8,128)(2,1)} %gather_fusion) | data formatting | bytes 8388608 | tf_op jit(solution)/shard_map/jit(_take)/gather | solution.py:59
  135.3 7.2 %copy_select_fusion = bf16[128,2,8192]{2,0,1:T(8,128)(2,1)S(1)} fusion(bf16[128,2,8192]{2,1,0:T(2,128)(2,1)} %reshape.94, pred[128,2]{0,1:T(4,128)(4,1)S(1)} %get-tuple-element.250), kind=kLoop, calls=%fused_computation.47 | loop fusion | flops 2097152 | bytes 8388864 | tf_op jit(solution)/shard_map/jit(_take)/select_n | solution.py:59
  142.6 1.4 multiply_reduce_fusion
  144.0 3.0 multiply_convert_fusion.1
  147.1 205.3 %all-gather.2.cloned.1.call-done = bf16[2048,8192]{1,0:T(8,128)(2,1)} async-done(((bf16[128,8192]{1,0:T(8,128)(2,1)}), bf16[2048,8192]{1,0:T(8,128)(2,1)}) %all-gather.2.cloned.1.call-update) | async-done | bytes 33554448 | tf_op jit(solution)/shard_map/all_gather | solution.py:71
  352.4 23.7 %convolution_convert_fusion = bf16[2048,512]{1,0:T(8,128)(2,1)S(1)} fusion(bf16[2048,8192]{1,0:T(8,128)(2,1)} %all-gather.2.cloned.1.call-done, bf16[8192,512]{1,0:T(8,128)(2,1)} %param.24), kind=kOutput, calls=%fused_computation.52 | convolution fusion | flops 17180917760 | bytes 44040192 | tf_op jit(solution)/shard_map/dot_general | solution.py:70
  376.2 1.3 copy-done.4
  377.5 3.7 collective-permute-start.1
  382.0 6.0 multiply_convert_fusion
  388.0 1.8 fusion.34
  389.8 1.7 fusion.35
  391.5 3.6 reshape.109
  395.2 4.0 copy.57
  399.2 75.3 %all-reduce.4 = bf16[2048,128]{1,0:T(8,128)(2,1)S(1)} all-reduce(f32[2048,128]{1,0:T(8,128)} %fusion.35), channel_id=1, replica_groups=mesh['seq'=8,'exp'=16] {'exp'}, use_global_device_ids=true, to_apply=%region_1.2 | all-reduce | flops 262144 | bytes 1572864 | tf_op jit(solution)/shard_map/psum | solution.py:85
  475.5 1.2 copy.58
  477.9 38.5 %while.34 = (s32[]{:T(128)}, f32[8,64,64]{1,2,0:T(8,128)S(1)}, f32[8]{0:T(128)S(1)}, f32[8,256,8]{1,2,0:T(8,128)}, f32[8,256,8,64]{1,3,2,0:T(8,128)}, /*index=5*...) while((s32[]{:T(128)}, f32[8,64,64]{1,2,0:T(8,128)S(1)}, ...), condition=%wide.region_6.7_spmd.clone, body=%wide.region_3.6_spmd.clone.sunk | while | flops 180033568 | bytes 2758157 | solution.py:111
  479.3 1.6 fusion.62
  484.1 1.6 fusion.62
  488.9 1.6 fusion.62
  493.7 1.6 fusion.62
  498.5 1.6 fusion.62
  503.3 1.6 fusion.62
  508.1 1.6 fusion.62
  513.0 1.5 fusion.62
  516.6 71.0 %while.33 = (s32[]{:T(128)}, f32[8,64,64]{2,1,0:T(8,128)}, f32[8,64,64]{2,1,0:T(8,128)S(1)}, f32[8]{0:T(128)S(1)}, f32[8,64,64]{2,1,0:T(8,128)S(1)}, /*index=5*/s32[]{:T(128)}) while((s32[]{:T(128)}, f32[8,64,64]{2,1,0:T(8,128)}, f32[8,64,64]{2,1,0:T(8,128)S(1)}, f32[8]{0:T(128)S(1)}, f32[8,64,64]{2,1,0:T(8,128)S(1)}, ...), condition=%wide.region_8.9_spmd, body=%wide.region_7.8_spmd.sunk | while | flops 65538 | bytes 1441961 | solution.py:129
  516.6 16.7 %collective-permute-start = (f32[8,64,64]{2,1,0:T(8,128)S(1)}, f32[8,64,64]{2,1,0:T(8,128)S(1)}, u32[]{:S(2)}, u32[]{:S(2)}) collective-permute-start(f32[8,64,64]{2,1,0:T(8,128)S(1)} %get-tuple-element.428), channel_id=1, source_target_pairs={{0,16},{16,32},{32,48},{48,64},{64,80},{80,96},{96,112},{1,17},{17... | collective-permute-start | bytes 393224 | tf_op jit(solution)/shard_map/while/body/eval_jaxpr/ppermute | solution.py:16
  533.3 3.3 collective-permute-done
  537.3 4.4 collective-permute-start
  541.7 3.3 collective-permute-done
  545.7 4.4 collective-permute-start
  550.1 3.3 collective-permute-done
  554.1 4.4 collective-permute-start
  558.5 3.3 collective-permute-done
  562.5 4.4 collective-permute-start
  566.8 3.3 collective-permute-done
  570.8 4.4 collective-permute-start
  575.2 3.3 collective-permute-done
  579.2 4.4 collective-permute-start
  583.6 3.3 collective-permute-done
  587.6 1.1 copy.61
  588.7 1.8 multiply_add_fusion.1
  590.5 1.8 fusion.36
  592.7 2.8 add_convert_fusion
  595.6 5.1 copy.67
  600.6 6.4 %reshape.108 = bf16[2048,512]{1,0:T(8,128)(2,1)} reshape(bf16[8,256,8,64]{3,2,1,0:T(8,128)(2,1)} %copy.67) | data formatting | bytes 4194304 | tf_op jit(solution)/shard_map/reshape | solution.py:137
  (197 shorter events, 34.4 us)
Async XLA Ops:
  6.5 381.5 %copy-start = (bf16[512,128]{1,0:T(8,128)(2,1)S(1)}, bf16[512,128]{1,0:T(8,128)(2,1)}, u32[]{:S(2)}) copy-start(bf16[512,128]{1,0:T(8,128)(2,1)} %param.28) | copy-start | bytes 393220
  6.5 7.8 %copy-start.10 = (s32[128,2]{0,1:T(2,128)S(1)}, s32[128,2]{0,1:T(2,128)}, u32[]{:S(2)}) copy-start(s32[128,2]{0,1:T(2,128)} %param.21) | copy-start | bytes 3076
  6.5 7.8 %copy-start.11 = (s32[128,2]{0,1:T(2,128)S(1)}, s32[128,2]{0,1:T(2,128)}, u32[]{:S(2)}) copy-start(s32[128,2]{0,1:T(2,128)} %param.20) | copy-start | bytes 3076
  6.5 8.1 %copy-start.12 = (f32[128,2]{0,1:T(2,128)S(1)}, f32[128,2]{0,1:T(2,128)}, u32[]{:S(2)}) copy-start(f32[128,2]{0,1:T(2,128)} %param.22) | copy-start | bytes 3076
  6.5 108.6 %all-to-all-start = ((bf16[1,1,16,24,8192]{4,3,1,0,2:T(8,128)(2,1)}), bf16[1,1,16,24,8192]{4,3,1,0,2:T(8,128)(2,1)}, u32[]{:S(2)}, u32[]{:S(2)}) async-start(bf16[1,1,16,24,8192]{4,3,1,0,2:T(8,128)(2,1)} %bitcast.113), calls=%async_computation | async-start | bytes 12582912 | tf_op jit(solution)/shard_map/all_to_all | solution.py:56
  14.3 338.1 %all-gather.2.cloned.1.call-start = ((), (), s32[]{:S(2)}) async-start(), calls=%async_computation.1 | async-start | bytes 35651584 | tf_op jit(solution)/shard_map/all_gather | solution.py:71
  135.3 7.2 %copy-start.2 = (bf16[128,8192]{1,0:T(8,128)(2,1)S(1)}, bf16[128,8192]{1,0:T(8,128)(2,1)}, u32[]{:S(2)}) copy-start(bf16[128,8192]{1,0:T(8,128)(2,1)} %param.18) | copy-start | bytes 6291460
  142.5 1.4 copy-start.7
  144.0 3.1 copy-start.8
  147.0 330.0 %all-reduce.3.cloned.1.call-start = ((), (), s32[]{:S(2)}) async-start(), calls=%async_computation.2 | async-start | bytes 2097152 | tf_op jit(solution)/shard_map/psum | solution.py:85
  147.1 234.2 %copy-start.15 = (f32[8]{0:T(128)S(1)}, f32[8]{0:T(128)}, u32[]{:S(2)}) copy-start(f32[8]{0:T(128)} %param.30) | copy-start | bytes 100
  147.1 234.9 %copy-start.9 = (f32[512]{0:T(512)S(1)}, f32[512]{0:T(512)}, u32[]{:S(2)}) copy-start(f32[512]{0:T(512)} %param.26) | copy-start | bytes 6148
  376.2 1.3 copy-start.4
  377.5 4.5 collective-permute-start.1
  382.0 7.8 %copy-start.5 = (bf16[512,128]{1,0:T(8,128)(2,1)S(1)}, bf16[512,128]{1,0:T(8,128)(2,1)}, u32[]{:S(2)}) copy-start(bf16[512,128]{1,0:T(8,128)(2,1)} %param.27) | copy-start | bytes 393220
  395.2 81.8 %copy-start.13 = (f32[8]{0:T(128)S(1)}, f32[8]{0:T(128)}, u32[]{:S(2)}) copy-start(f32[8]{0:T(128)} %param.29) | copy-start | bytes 100
  516.6 20.0 %collective-permute-start = (f32[8,64,64]{2,1,0:T(8,128)S(1)}, f32[8,64,64]{2,1,0:T(8,128)S(1)}, u32[]{:S(2)}, u32[]{:S(2)}) collective-permute-start(f32[8,64,64]{2,1,0:T(8,128)S(1)} %get-tuple-element.428), channel_id=1, source_target_pairs={{0,16},{16,32},{32,48},{48,64},{64,80},{80,96},{96,112},{1,17},{17... | collective-permute-start | bytes 393224 | tf_op jit(solution)/shard_map/while/body/eval_jaxpr/ppermute | solution.py:16
  536.6 0.7 copy-start.1
  537.3 7.7 %collective-permute-start = (f32[8,64,64]{2,1,0:T(8,128)S(1)}, f32[8,64,64]{2,1,0:T(8,128)S(1)}, u32[]{:S(2)}, u32[]{:S(2)}) collective-permute-start(f32[8,64,64]{2,1,0:T(8,128)S(1)} %get-tuple-element.428), channel_id=1, source_target_pairs={{0,16},{16,32},{32,48},{48,64},{64,80},{80,96},{96,112},{1,17},{17... | collective-permute-start | bytes 393224 | tf_op jit(solution)/shard_map/while/body/eval_jaxpr/ppermute | solution.py:16
  545.0 0.7 copy-start.1
  545.7 7.7 %collective-permute-start = (f32[8,64,64]{2,1,0:T(8,128)S(1)}, f32[8,64,64]{2,1,0:T(8,128)S(1)}, u32[]{:S(2)}, u32[]{:S(2)}) collective-permute-start(f32[8,64,64]{2,1,0:T(8,128)S(1)} %get-tuple-element.428), channel_id=1, source_target_pairs={{0,16},{16,32},{32,48},{48,64},{64,80},{80,96},{96,112},{1,17},{17... | collective-permute-start | bytes 393224 | tf_op jit(solution)/shard_map/while/body/eval_jaxpr/ppermute | solution.py:16
  553.4 0.7 copy-start.1
  554.1 7.7 %collective-permute-start = (f32[8,64,64]{2,1,0:T(8,128)S(1)}, f32[8,64,64]{2,1,0:T(8,128)S(1)}, u32[]{:S(2)}, u32[]{:S(2)}) collective-permute-start(f32[8,64,64]{2,1,0:T(8,128)S(1)} %get-tuple-element.428), channel_id=1, source_target_pairs={{0,16},{16,32},{32,48},{48,64},{64,80},{80,96},{96,112},{1,17},{17... | collective-permute-start | bytes 393224 | tf_op jit(solution)/shard_map/while/body/eval_jaxpr/ppermute | solution.py:16
  561.8 0.7 copy-start.1
  562.5 7.7 %collective-permute-start = (f32[8,64,64]{2,1,0:T(8,128)S(1)}, f32[8,64,64]{2,1,0:T(8,128)S(1)}, u32[]{:S(2)}, u32[]{:S(2)}) collective-permute-start(f32[8,64,64]{2,1,0:T(8,128)S(1)} %get-tuple-element.428), channel_id=1, source_target_pairs={{0,16},{16,32},{32,48},{48,64},{64,80},{80,96},{96,112},{1,17},{17... | collective-permute-start | bytes 393224 | tf_op jit(solution)/shard_map/while/body/eval_jaxpr/ppermute | solution.py:16
  570.1 0.7 copy-start.1
  570.8 7.7 %collective-permute-start = (f32[8,64,64]{2,1,0:T(8,128)S(1)}, f32[8,64,64]{2,1,0:T(8,128)S(1)}, u32[]{:S(2)}, u32[]{:S(2)}) collective-permute-start(f32[8,64,64]{2,1,0:T(8,128)S(1)} %get-tuple-element.428), channel_id=1, source_target_pairs={{0,16},{16,32},{32,48},{48,64},{64,80},{80,96},{96,112},{1,17},{17... | collective-permute-start | bytes 393224 | tf_op jit(solution)/shard_map/while/body/eval_jaxpr/ppermute | solution.py:16
  578.5 0.7 copy-start.1
  579.2 7.7 %collective-permute-start = (f32[8,64,64]{2,1,0:T(8,128)S(1)}, f32[8,64,64]{2,1,0:T(8,128)S(1)}, u32[]{:S(2)}, u32[]{:S(2)}) collective-permute-start(f32[8,64,64]{2,1,0:T(8,128)S(1)} %get-tuple-element.428), channel_id=1, source_target_pairs={{0,16},{16,32},{32,48},{48,64},{64,80},{80,96},{96,112},{1,17},{17... | collective-permute-start | bytes 393224 | tf_op jit(solution)/shard_map/while/body/eval_jaxpr/ppermute | solution.py:16
  586.9 0.7 copy-start.1
  590.5 1.9 copy-start.6
  590.5 2.2 copy-start.3
  590.5 2.2 copy-start.14
Sparse Core Ops, SparseCore 0:
  147.1 205.2 all-gather.1
  390.0 86.9 all-reduce.2
where the time goes:
time: 615 us; the launch traced here: 614 us
  waiting for transfers between devices  330 us (54%)
  blocking collectives  75.3 us (12%)
  starting transfers between devices  54.6 us (9%)
  local copies, waits for them, and re-layouts  52.2 us (8%)
  matrix products  46.7 us (8%)
  other arithmetic  41.4 us (7%)
  between operations  13.8 us (2%)
    all_gather x1, waiting for transfers between devices, shards(): lax.all_gather(normed, 'exp', axis=0, tiled=True)  205 us
    all_to_all x1, waiting for transfers between devices, shards(): lax.all_to_all(expert_rows, 'exp', split_axis=2, concat_axis=1, tiled=True)  100 us
    psum x1, blocking collectives, shards(): state_proj, dt_raw = lax.psum((state_part, rate_part), 'exp')  75.3 us
    ppermute x8, starting transfers between devices, passed_along(): lax.ppermute(value, axis, [(source, source + steps) for source in range(l...  46.7 us
    dot_general x1, matrix products, shards(): jnp.dot(lax.all_gather(normed, 'exp', axis=0, tiled=True), in_weight, pre...  23.7 us
    ppermute x8, waiting for transfers between devices, passed_along(): lax.ppermute(value, axis, [(source, source + steps) for source in range(l...  23.7 us
    gather x2, local copies, waits for them, and re-layouts, shards(): picked = jnp.take(buffers, expert_ids * capacity + expert_slots, axis=0)  20.2 us
    dot_general x8, matrix products, block_terms(): jnp.einsum('tsh,shp->thp', mixing, values, preferred_element_type=jnp.flo...  12.5 us
  transfers between devices with their start and end apart: 11, of which 11 were waited for; matrix products, arithmetic and copies ran while one was open for 2% of the time, Pallas kernels for 0%

commit v1 on v0

--- a/solution.py
+++ b/solution.py
@@ -8,6 +8,12 @@
 HEAD = 64
 NSTATE = 64
 STRETCH = 256
+
+
+def _treat_sides(xin, ndim_at):
+    a_now = list(xin.shape[1:])
+    a_now[ndim_at] *= xin.shape[0]
+    return jnp.moveaxis(xin, 0, ndim_at).reshape(a_now)
 
 
 def passed_along(value, axis, steps):
@@ -52,6 +58,28 @@
     decay_log,
     skip_gain,
 ):
+
+    def move_pieces_all_now(on_dim, t0, row_axis):
+        many = lax.axis_size(row_axis)
+        pile = tuple(((h, (h + 1) % many) for h in range(many)))
+        near, block_next = ([], [])
+        crops = tuple(((pp, nth) for nth, pp in pile))
+        for ix in [*range(many - 1)]:
+            if ix % 2 == 0:
+                t_next = lax.ppermute(near[-1] if near else t0, axis_name=row_axis, perm=pile)
+                near.append(t_next)
+            else:
+                inter = lax.ppermute(
+                    block_next[-1] if block_next else t0, axis_name=row_axis, perm=crops
+                )
+                block_next.append(inter)
+        upper = jnp.stack([*near[::-1], t0, *block_next], axis=0)
+        now = lax.axis_index(row_axis)
+        met_up = len(near)
+        r_now = now - met_up
+        upper = upper[(jnp.arange(many) - r_now) % many]
+        return _treat_sides(upper, on_dim)
+
     own_rows, width = residual.shape
     returned = lax.all_to_all(expert_rows, "exp", split_axis=2, concat_axis=1, tiled=True)
     capacity = returned.shape[3]
@@ -68,9 +96,7 @@
     group_rows = own_rows * lax.axis_size("exp")
     local_width = in_weight.shape[1]
     x_in = jnp.dot(
-        lax.all_gather(normed, "exp", axis=0, tiled=True),
-        in_weight,
-        preferred_element_type=jnp.float32,
+        move_pieces_all_now(0, normed, "exp"), in_weight, preferred_element_type=jnp.float32
     ).astype(jnp.bfloat16)
     rim_rows = passed_along(x_in[group_rows - (KCONV - 1) :], "seq", 1)
     padded = jnp.concatenate([rim_rows, x_in], axis=0)

time: 615 us -> 860 us (1.40)
  waiting for transfers between devices: 330 us -> 454 us
  local copies, waits for them, and re-layouts: 52.2 us -> 107 us
  starting transfers between devices: 54.6 us -> 94.4 us
  other arithmetic: 41.4 us -> 63 us
    ppermute x0 -> x15, waiting for transfers between devices: none -> 328 us  [the longest x8 328 us: move_pieces_all_now(): lax.ppermute(near[-1] if near else t0, axis_name=row_axis, perm=pile)]
    all_gather x1 -> x0, waiting for transfers between devices: 205 us -> none  [shards(): lax.all_gather(normed, 'exp', axis=0, tiled=True)]
    gather x0 -> x3, local copies, waits for them, and re-layouts: none -> 38 us  [move_pieces_all_now(): upper = upper[(jnp.arange(many) - r_now) % many]]
    ppermute x0 -> x15, starting transfers between devices: none -> 34 us  [the longest x7 33.9 us: move_pieces_all_now(): lax.ppermute(block_next[-1] if block_next else t0, axis_name=row_axis, pe...]
    unnamed x2 -> x3, other arithmetic: 0.01 us -> 22.8 us
    unnamed x33 -> x96, local copies, waits for them, and re-layouts: 7.01 us -> 23.1 us
  transfers between devices with their start and end apart: 11 -> 25, of which waited for: 11 -> 18; matrix products, arithmetic and copies ran while one was open for 2% -> 2% of each run, Pallas kernels for 0% -> 0%
where the time goes in v1:
time: 860 us; the launch traced here: 853 us
  waiting for transfers between devices  454 us (53%)
  local copies, waits for them, and re-layouts  107 us (12%)
  starting transfers between devices  94.4 us (11%)
  blocking collectives  73.2 us (9%)
  other arithmetic  63 us (7%)
  matrix products  46.6 us (5%)
  between operations  14.3 us (2%)
    ppermute x8, waiting for transfers between devices, move_pieces_all_now(): lax.ppermute(near[-1] if near else t0, axis_name=row_axis, perm=pile)  328 us
    all_to_all x1, waiting for transfers between devices, shards(): lax.all_to_all(expert_rows, 'exp', split_axis=2, concat_axis=1, tiled=True)  100 us
    psum x1, blocking collectives, shards(): state_proj, dt_raw = lax.psum((state_part, rate_part), 'exp')  73.2 us
    ppermute x8, starting transfers between devices, passed_along(): lax.ppermute(value, axis, [(source, source + steps) for source in range(l...  52.7 us
    gather x3, local copies, waits for them, and re-layouts, move_pieces_all_now(): upper = upper[(jnp.arange(many) - r_now) % many]  38 us
    ppermute x7, starting transfers between devices, move_pieces_all_now(): lax.ppermute(block_next[-1] if block_next else t0, axis_name=row_axis, pe...  33.9 us
    dot_general x1, matrix products, shards(): jnp.dot(move_pieces_all_now(0, normed, 'exp'), in_weight, preferred_eleme...  23.8 us
    ppermute x8, waiting for transfers between devices, passed_along(): lax.ppermute(value, axis, [(source, source + steps) for source in range(l...  23.5 us
  transfers between devices with their start and end apart: 25, of which 18 were waited for; matrix products, arithmetic and copies ran while one was open for 2% of the time, Pallas kernels for 0%

profile of v1, /device:TPU:1, one launch (start us, length us, event | category | flops | bytes accessed | tf_op | source)
XLA Modules:
  0.0 853.2 jit_solution(3768130091586845297)
XLA Ops:
  6.5 7.8 all-to-all-start
  14.7 100.4 %all-to-all-done = bf16[1,1,16,24,8192]{4,3,1,0,2:T(8,128)(2,1)} async-done(((bf16[1,1,16,24,8192]{4,3,1,0,2:T(8,128)(2,1)}), bf16[1,1,16,24,8192]{4,3,1,0,2:T(8,128)(2,1)}, u32[]{:S(2)}, u32[]{:S(2)}) %all-to-all-start) | async-done | bytes 6291488 | tf_op jit(solution)/shard_map/all_to_all | solution.py:84
  115.1 12.7 %gather_fusion = bf16[256,8192]{1,0:T(8,128)(2,1)} fusion(bf16[384,8192]{1,0:T(8,128)(2,1)} %bitcast.3, s32[1024]{0:T(1024)S(1)} %pad_clamp_fusion.1), kind=kCustom, calls=%fused_computation | custom fusion | bytes 8389632 | tf_op jit(solution)/shard_map/jit(_take)/gather | solution.py:87
  127.8 8.1 reshape.147
  135.8 7.2 copy_select_fusion
  146.4 48.0 %collective-permute-done.1 = bf16[128,8192]{1,0:T(8,128)(2,1)S(1)} collective-permute-done((bf16[128,8192]{1,0:T(8,128)(2,1)S(1)}, bf16[128,8192]{1,0:T(8,128)(2,1)S(1)}, u32[]{:S(2)}, u32[]{:S(2)}) %collective-permute-start.1) | collective-permute-done | bytes 2097184 | tf_op jit(solution)/shard_map/ppermute | solution.py:69
  194.4 4.8 collective-permute-start.9
  199.1 42.3 %collective-permute-done.2 = bf16[128,8192]{1,0:T(8,128)(2,1)S(1)} collective-permute-done((bf16[128,8192]{1,0:T(8,128)(2,1)S(1)}, bf16[128,8192]{1,0:T(8,128)(2,1)S(1)}, u32[]{:S(2)}, u32[]{:S(2)}) %collective-permute-start.2) | collective-permute-done | bytes 2097184 | tf_op jit(solution)/shard_map/ppermute | solution.py:69
  241.4 4.8 collective-permute-start.10
  246.3 41.3 %collective-permute-done.3 = bf16[128,8192]{1,0:T(8,128)(2,1)S(1)} collective-permute-done((bf16[128,8192]{1,0:T(8,128)(2,1)S(1)}, bf16[128,8192]{1,0:T(8,128)(2,1)S(1)}, u32[]{:S(2)}, u32[]{:S(2)}) %collective-permute-start.3) | collective-permute-done | bytes 2097184 | tf_op jit(solution)/shard_map/ppermute | solution.py:69
  287.5 4.8 collective-permute-start.11
  292.4 40.3 %collective-permute-done.4 = bf16[128,8192]{1,0:T(8,128)(2,1)S(1)} collective-permute-done((bf16[128,8192]{1,0:T(8,128)(2,1)S(1)}, bf16[128,8192]{1,0:T(8,128)(2,1)S(1)}, u32[]{:S(2)}, u32[]{:S(2)}) %collective-permute-start.4) | collective-permute-done | bytes 2097184 | tf_op jit(solution)/shard_map/ppermute | solution.py:69
  332.7 5.0 collective-permute-start.12
  337.8 39.2 %collective-permute-done.5 = bf16[128,8192]{1,0:T(8,128)(2,1)S(1)} collective-permute-done((bf16[128,8192]{1,0:T(8,128)(2,1)S(1)}, bf16[128,8192]{1,0:T(8,128)(2,1)S(1)}, u32[]{:S(2)}, u32[]{:S(2)}) %collective-permute-start.5) | collective-permute-done | bytes 2097184 | tf_op jit(solution)/shard_map/ppermute | solution.py:69
  378.3 4.8 collective-permute-start.13
  383.1 38.0 %collective-permute-done.6 = bf16[128,8192]{1,0:T(8,128)(2,1)S(1)} collective-permute-done((bf16[128,8192]{1,0:T(8,128)(2,1)S(1)}, bf16[128,8192]{1,0:T(8,128)(2,1)S(1)}, u32[]{:S(2)}, u32[]{:S(2)}) %collective-permute-start.6) | collective-permute-done | bytes 2097184 | tf_op jit(solution)/shard_map/ppermute | solution.py:69
  421.1 4.8 collective-permute-start.14
  425.9 39.3 %collective-permute-done.7 = bf16[128,8192]{1,0:T(8,128)(2,1)} collective-permute-done((bf16[128,8192]{1,0:T(8,128)(2,1)S(1)}, bf16[128,8192]{1,0:T(8,128)(2,1)}, u32[]{:S(2)}, u32[]{:S(2)}) %collective-permute-start.7) | collective-permute-done | bytes 2097184 | tf_op jit(solution)/shard_map/ppermute | solution.py:69
  465.4 4.9 collective-permute-start.15
  470.2 39.2 %collective-permute-done.8 = bf16[128,8192]{1,0:T(8,128)(2,1)} collective-permute-done((bf16[128,8192]{1,0:T(8,128)(2,1)}, bf16[128,8192]{1,0:T(8,128)(2,1)}, u32[]{:S(2)}, u32[]{:S(2)}) %collective-permute-start.8) | collective-permute-done | bytes 2097184 | tf_op jit(solution)/shard_map/ppermute | solution.py:69
  524.4 11.8 %fusion.34 = (bf16[16,128,4096]{2,1,0:T(8,128)(2,1)}, bf16[16,128,4096]{2,1,0:T(8,128)(2,1)}) fusion(bf16[16,128,8192]{2,1,0:T(8,128)(2,1)S(1)} %bitcast_dynamic-update-slice_fusion.2), kind=kLoop, calls=%fused_computation.96 | loop fusion | bytes 67108864 | tf_op jit(solution)/shard_map/gather | solution.py:80
  536.2 13.1 %gather_fusion.1 = bf16[16,128,4096]{2,1,0:T(8,128)(2,1)} fusion(bf16[16,128,4096]{2,1,0:T(8,128)(2,1)} %get-tuple-element.255, s32[1024]{0:T(1024)S(1)} %pad_clamp_fusion), kind=kCustom, calls=%fused_computation.1 | custom fusion | bytes 33554496 | tf_op jit(solution)/shard_map/gather | solution.py:80
  549.3 13.1 %gather_fusion.2 = bf16[16,128,4096]{2,1,0:T(8,128)(2,1)} fusion(bf16[16,128,4096]{2,1,0:T(8,128)(2,1)} %get-tuple-element.256, s32[1024]{0:T(1024)S(1)} %pad_clamp_fusion), kind=kCustom, calls=%fused_computation.2 | custom fusion | bytes 33554496 | tf_op jit(solution)/shard_map/gather | solution.py:80
  562.4 22.8 %pad_maximum_fusion = bf16[16,128,8192]{2,1,0:T(8,128)(2,1)} fusion(bf16[16,128,4096]{2,1,0:T(8,128)(2,1)} %gather_fusion.2, bf16[16,128,4096]{2,1,0:T(8,128)(2,1)} %gather_fusion.1), kind=kLoop, calls=%fused_computation.45 | loop fusion | flops 67108864 | bytes 67108864
  585.2 23.8 %convolution_convert_fusion = bf16[2048,512]{1,0:T(8,128)(2,1)S(1)} fusion(bf16[2048,8192]{1,0:T(8,128)(2,1)} %bitcast.146, bf16[8192,512]{1,0:T(8,128)(2,1)} %param.24), kind=kOutput, calls=%fused_computation.55 | convolution fusion | flops 17180917760 | bytes 44040192 | tf_op jit(solution)/shard_map/dot_general | solution.py:98
  610.3 13.3 %collective-permute-start.16 = (bf16[3,512]{1,0:T(4,128)(2,1)S(1)}, bf16[3,512]{1,0:T(4,128)(2,1)S(1)}, u32[]{:S(2)}, u32[]{:S(2)}) collective-permute-start(bf16[3,512]{1,0:T(4,128)(2,1)S(1)} %slice.81), channel_id=1, source_target_pairs={{0,16},{16,32},{32,48},{48,64},{64,80},{80,96},{96,112},{1,17},{17... | collective-permute-start | bytes 9224 | tf_op jit(solution)/shard_map/ppermute | solution.py:22
  624.1 6.0 multiply_convert_fusion
  633.6 3.7 reshape.178
  637.3 4.0 copy.57
  641.3 73.2 %all-reduce.4 = bf16[2048,128]{1,0:T(8,128)(2,1)S(1)} all-reduce(f32[2048,128]{1,0:T(8,128)} %fusion.38), channel_id=1, replica_groups=mesh['seq'=8,'exp'=16] {'exp'}, use_global_device_ids=true, to_apply=%region_1.2 | all-reduce | flops 262144 | bytes 1572864 | tf_op jit(solution)/shard_map/psum | solution.py:111
  720.6 38.5 %while.34 = (s32[]{:T(128)}, f32[8,64,64]{1,2,0:T(8,128)S(1)}, f32[8]{0:T(128)S(1)}, f32[8,256,8]{1,2,0:T(8,128)}, f32[8,256,8,64]{1,3,2,0:T(8,128)}, /*index=5*...) while((s32[]{:T(128)}, f32[8,64,64]{1,2,0:T(8,128)S(1)}, ...), condition=%wide.region_6.7_spmd.clone, body=%wide.region_3.6_spmd.clone.sunk | while | flops 180033568 | bytes 2758157 | solution.py:137
  759.3 67.4 %while.33 = (s32[]{:T(128)}, f32[8,64,64]{2,1,0:T(8,128)}, f32[8,64,64]{2,1,0:T(8,128)S(1)}, f32[8]{0:T(128)S(1)}, f32[8,64,64]{2,1,0:T(8,128)S(1)}, /*index=5*/s32[]{:T(128)}) while((s32[]{:T(128)}, f32[8,64,64]{2,1,0:T(8,128)}, f32[8,64,64]{2,1,0:T(8,128)S(1)}, f32[8]{0:T(128)S(1)}, f32[8,64,64]{2,1,0:T(8,128)S(1)}, ...), condition=%wide.region_8.9_spmd, body=%wide.region_7.8_spmd.sunk | while | flops 65538 | bytes 1441961 | solution.py:155
  759.3 13.1 %collective-permute-start = (f32[8,64,64]{2,1,0:T(8,128)S(1)}, f32[8,64,64]{2,1,0:T(8,128)S(1)}, u32[]{:S(2)}, u32[]{:S(2)}) collective-permute-start(f32[8,64,64]{2,1,0:T(8,128)S(1)} %get-tuple-element.430), channel_id=1, source_target_pairs={{0,16},{16,32},{32,48},{48,64},{64,80},{80,96},{96,112},{1,17},{17... | collective-permute-start | bytes 393224 | tf_op jit(solution)/shard_map/while/body/eval_jaxpr/ppermute | solution.py:22
  772.4 3.3 collective-permute-done
  776.4 4.4 collective-permute-start
  780.8 3.3 collective-permute-done
  784.8 4.4 collective-permute-start
  789.2 3.3 collective-permute-done
  793.1 4.4 collective-permute-start
  797.5 3.3 collective-permute-done
  801.5 4.4 collective-permute-start
  805.9 3.3 collective-permute-done
  809.9 4.4 collective-permute-start
  814.3 3.3 collective-permute-done
  818.3 4.4 collective-permute-start
  822.6 3.3 collective-permute-done
  834.6 5.1 copy.67
  839.7 6.4 reshape.177
  (294 shorter events, 82.4 us)
Async XLA Ops:
  6.5 623.6 %copy-start = (bf16[512,128]{1,0:T(8,128)(2,1)S(1)}, bf16[512,128]{1,0:T(8,128)(2,1)}, u32[]{:S(2)}) copy-start(bf16[512,128]{1,0:T(8,128)(2,1)} %param.28) | copy-start | bytes 393220
  6.5 7.8 copy-start.34
  6.5 7.8 copy-start.35
  6.5 8.1 copy-start.36
  6.5 108.6 %all-to-all-start = ((bf16[1,1,16,24,8192]{4,3,1,0,2:T(8,128)(2,1)}), bf16[1,1,16,24,8192]{4,3,1,0,2:T(8,128)(2,1)}, u32[]{:S(2)}, u32[]{:S(2)}) async-start(bf16[1,1,16,24,8192]{4,3,1,0,2:T(8,128)(2,1)} %bitcast.149), calls=%async_computation | async-start | bytes 12582912 | tf_op jit(solution)/shard_map/all_to_all | solution.py:84
  14.3 705.3 %all-reduce.3.cloned.1.call-start = ((), (), s32[]{:S(2)}) async-start(), calls=%async_computation.1 | async-start | bytes 2097152 | tf_op jit(solution)/shard_map/psum | solution.py:111
  135.8 7.2 copy-start.2
  144.4 320.9 %copy-start.32 = (f32[4,512]{1,0:T(4,128)S(1)}, f32[4,512]{1,0:T(4,128)}, u32[]{:S(2)}) copy-start(f32[4,512]{1,0:T(4,128)} %param.25) | copy-start | bytes 24580
  146.3 48.1 %copy-start.3 = (bf16[128,8192]{1,0:T(8,128)(2,1)}, bf16[128,8192]{1,0:T(8,128)(2,1)S(1)}, u32[]{:S(2)}) copy-start(bf16[128,8192]{1,0:T(8,128)(2,1)S(1)} %multiply_convert_fusion.1) | copy-start | bytes 6291460
  146.3 48.0 %collective-permute-start.1 = (bf16[128,8192]{1,0:T(8,128)(2,1)S(1)}, bf16[128,8192]{1,0:T(8,128)(2,1)S(1)}, u32[]{:S(2)}, u32[]{:S(2)}) collective-permute-start(bf16[128,8192]{1,0:T(8,128)(2,1)S(1)} %multiply_convert_fusion.1), channel_id=1, source_target_pairs={{0,1},{1,2},{2,3},{3,4},{4,5},{5,6},{6,7},{7,8},{8,9},{9,10},{10,1... | collective-permute-start | bytes 6291464 | tf_op jit(solution)/shard_map/ppermute | solution.py:69
  194.3 47.1 %copy-start.7 = (bf16[128,8192]{1,0:T(8,128)(2,1)}, bf16[128,8192]{1,0:T(8,128)(2,1)S(1)}, u32[]{:S(2)}) copy-start(bf16[128,8192]{1,0:T(8,128)(2,1)S(1)} %collective-permute-done.1) | copy-start | bytes 6291460
  194.3 47.0 %collective-permute-start.2 = (bf16[128,8192]{1,0:T(8,128)(2,1)S(1)}, bf16[128,8192]{1,0:T(8,128)(2,1)S(1)}, u32[]{:S(2)}, u32[]{:S(2)}) collective-permute-start(bf16[128,8192]{1,0:T(8,128)(2,1)S(1)} %collective-permute-done.1), channel_id=1, source_target_pairs={{0,1},{1,2},{2,3},{3,4},{4,5},{5,6},{6,7},{7,8},{8,9},{9,10},{10,1... | collective-permute-start | bytes 6291464 | tf_op jit(solution)/shard_map/ppermute | solution.py:69
  194.4 47.0 %collective-permute-start.9 = (bf16[128,8192]{1,0:T(8,128)(2,1)S(1)}, bf16[128,8192]{1,0:T(8,128)(2,1)S(1)}, u32[]{:S(2)}, u32[]{:S(2)}) collective-permute-start(bf16[128,8192]{1,0:T(8,128)(2,1)S(1)} %multiply_convert_fusion.1), channel_id=1, source_target_pairs={{1,0},{2,1},{3,2},{4,3},{5,4},{6,5},{7,6},{8,7},{9,8},{10,9},{11,1... | collective-permute-start | bytes 6291464 | tf_op jit(solution)/shard_map/ppermute | solution.py:72
  241.4 46.1 %copy-start.11 = (bf16[128,8192]{1,0:T(8,128)(2,1)}, bf16[128,8192]{1,0:T(8,128)(2,1)S(1)}, u32[]{:S(2)}) copy-start(bf16[128,8192]{1,0:T(8,128)(2,1)S(1)} %collective-permute-done.2) | copy-start | bytes 6291460
  241.4 46.1 %collective-permute-start.3 = (bf16[128,8192]{1,0:T(8,128)(2,1)S(1)}, bf16[128,8192]{1,0:T(8,128)(2,1)S(1)}, u32[]{:S(2)}, u32[]{:S(2)}) collective-permute-start(bf16[128,8192]{1,0:T(8,128)(2,1)S(1)} %collective-permute-done.2), channel_id=1, source_target_pairs={{0,1},{1,2},{2,3},{3,4},{4,5},{5,6},{6,7},{7,8},{8,9},{9,10},{10,1... | collective-permute-start | bytes 6291464 | tf_op jit(solution)/shard_map/ppermute | solution.py:69
  241.4 4.8 copy-start.9
  241.4 46.1 %collective-permute-start.10 = (bf16[128,8192]{1,0:T(8,128)(2,1)S(1)}, bf16[128,8192]{1,0:T(8,128)(2,1)S(1)}, u32[]{:S(2)}, u32[]{:S(2)}) collective-permute-start(bf16[128,8192]{1,0:T(8,128)(2,1)S(1)} %collective-permute-done.9), channel_id=1, source_target_pairs={{1,0},{2,1},{3,2},{4,3},{5,4},{6,5},{7,6},{8,7},{9,8},{10,9},{11,1... | collective-permute-start | bytes 6291464 | tf_op jit(solution)/shard_map/ppermute | solution.py:72
  287.5 45.2 %copy-start.15 = (bf16[128,8192]{1,0:T(8,128)(2,1)}, bf16[128,8192]{1,0:T(8,128)(2,1)S(1)}, u32[]{:S(2)}) copy-start(bf16[128,8192]{1,0:T(8,128)(2,1)S(1)} %collective-permute-done.3) | copy-start | bytes 6291460
  287.5 45.2 %collective-permute-start.4 = (bf16[128,8192]{1,0:T(8,128)(2,1)S(1)}, bf16[128,8192]{1,0:T(8,128)(2,1)S(1)}, u32[]{:S(2)}, u32[]{:S(2)}) collective-permute-start(bf16[128,8192]{1,0:T(8,128)(2,1)S(1)} %collective-permute-done.3), channel_id=1, source_target_pairs={{0,1},{1,2},{2,3},{3,4},{4,5},{5,6},{6,7},{7,8},{8,9},{9,10},{10,1... | collective-permute-start | bytes 6291464 | tf_op jit(solution)/shard_map/ppermute | solution.py:69
  287.5 4.8 copy-start.13
  287.5 45.2 %collective-permute-start.11 = (bf16[128,8192]{1,0:T(8,128)(2,1)S(1)}, bf16[128,8192]{1,0:T(8,128)(2,1)S(1)}, u32[]{:S(2)}, u32[]{:S(2)}) collective-permute-start(bf16[128,8192]{1,0:T(8,128)(2,1)S(1)} %collective-permute-done.10), channel_id=1, source_target_pairs={{1,0},{2,1},{3,2},{4,3},{5,4},{6,5},{7,6},{8,7},{9,8},{10,9},{11,1... | collective-permute-start | bytes 6291464 | tf_op jit(solution)/shard_map/ppermute | solution.py:72
  332.7 88.4 %copy-start.21 = (bf16[128,8192]{1,0:T(8,128)(2,1)}, bf16[128,8192]{1,0:T(8,128)(2,1)S(1)}, u32[]{:S(2)}) copy-start(bf16[128,8192]{1,0:T(8,128)(2,1)S(1)} %collective-permute-done.4) | copy-start | bytes 6291460
  332.7 44.3 %collective-permute-start.5 = (bf16[128,8192]{1,0:T(8,128)(2,1)S(1)}, bf16[128,8192]{1,0:T(8,128)(2,1)S(1)}, u32[]{:S(2)}, u32[]{:S(2)}) collective-permute-start(bf16[128,8192]{1,0:T(8,128)(2,1)S(1)} %collective-permute-done.4), channel_id=1, source_target_pairs={{0,1},{1,2},{2,3},{3,4},{4,5},{5,6},{6,7},{7,8},{8,9},{9,10},{10,1... | collective-permute-start | bytes 6291464 | tf_op jit(solution)/shard_map/ppermute | solution.py:69
  332.7 5.0 copy-start.17
  332.7 44.3 %collective-permute-start.12 = (bf16[128,8192]{1,0:T(8,128)(2,1)S(1)}, bf16[128,8192]{1,0:T(8,128)(2,1)S(1)}, u32[]{:S(2)}, u32[]{:S(2)}) collective-permute-start(bf16[128,8192]{1,0:T(8,128)(2,1)S(1)} %collective-permute-done.11), channel_id=1, source_target_pairs={{1,0},{2,1},{3,2},{4,3},{5,4},{6,5},{7,6},{8,7},{9,8},{10,9},{11,1... | collective-permute-start | bytes 6291464 | tf_op jit(solution)/shard_map/ppermute | solution.py:72
  377.0 48.9 %copy-start.25 = (bf16[128,8192]{1,0:T(8,128)(2,1)}, bf16[128,8192]{1,0:T(8,128)(2,1)S(1)}, u32[]{:S(2)}) copy-start(bf16[128,8192]{1,0:T(8,128)(2,1)S(1)} %collective-permute-done.5) | copy-start | bytes 6291460
  377.0 44.1 %collective-permute-start.6 = (bf16[128,8192]{1,0:T(8,128)(2,1)S(1)}, bf16[128,8192]{1,0:T(8,128)(2,1)S(1)}, u32[]{:S(2)}, u32[]{:S(2)}) collective-permute-start(bf16[128,8192]{1,0:T(8,128)(2,1)S(1)} %collective-permute-done.5), channel_id=1, source_target_pairs={{0,1},{1,2},{2,3},{3,4},{4,5},{5,6},{6,7},{7,8},{8,9},{9,10},{10,1... | collective-permute-start | bytes 6291464 | tf_op jit(solution)/shard_map/ppermute | solution.py:69
  378.3 42.8 %collective-permute-start.13 = (bf16[128,8192]{1,0:T(8,128)(2,1)S(1)}, bf16[128,8192]{1,0:T(8,128)(2,1)S(1)}, u32[]{:S(2)}, u32[]{:S(2)}) collective-permute-start(bf16[128,8192]{1,0:T(8,128)(2,1)S(1)} %collective-permute-done.12), channel_id=1, source_target_pairs={{1,0},{2,1},{3,2},{4,3},{5,4},{6,5},{7,6},{8,7},{9,8},{10,9},{11,1... | collective-permute-start | bytes 6291464 | tf_op jit(solution)/shard_map/ppermute | solution.py:72
  421.1 44.2 %copy-start.27 = (bf16[128,8192]{1,0:T(8,128)(2,1)}, bf16[128,8192]{1,0:T(8,128)(2,1)S(1)}, u32[]{:S(2)}) copy-start(bf16[128,8192]{1,0:T(8,128)(2,1)S(1)} %collective-permute-done.6) | copy-start | bytes 6291460
  421.1 44.2 %collective-permute-start.7 = (bf16[128,8192]{1,0:T(8,128)(2,1)S(1)}, bf16[128,8192]{1,0:T(8,128)(2,1)}, u32[]{:S(2)}, u32[]{:S(2)}) collective-permute-start(bf16[128,8192]{1,0:T(8,128)(2,1)S(1)} %collective-permute-done.6), channel_id=1, source_target_pairs={{0,1},{1,2},{2,3},{3,4},{4,5},{5,6},{6,7},{7,8},{8,9},{9,10},{10,1... | collective-permute-start | bytes 6291464 | tf_op jit(solution)/shard_map/ppermute | solution.py:69
  421.1 49.1 %copy-start.23 = (bf16[128,8192]{1,0:T(8,128)(2,1)}, bf16[128,8192]{1,0:T(8,128)(2,1)S(1)}, u32[]{:S(2)}) copy-start(bf16[128,8192]{1,0:T(8,128)(2,1)S(1)} %collective-permute-done.13) | copy-start | bytes 6291460
  421.1 44.2 %collective-permute-start.14 = (bf16[128,8192]{1,0:T(8,128)(2,1)S(1)}, bf16[128,8192]{1,0:T(8,128)(2,1)}, u32[]{:S(2)}, u32[]{:S(2)}) collective-permute-start(bf16[128,8192]{1,0:T(8,128)(2,1)S(1)} %collective-permute-done.13), channel_id=1, source_target_pairs={{1,0},{2,1},{3,2},{4,3},{5,4},{6,5},{7,6},{8,7},{9,8},{10,9},{11,1... | collective-permute-start | bytes 6291464 | tf_op jit(solution)/shard_map/ppermute | solution.py:72
  465.3 44.1 %collective-permute-start.8 = (bf16[128,8192]{1,0:T(8,128)(2,1)}, bf16[128,8192]{1,0:T(8,128)(2,1)}, u32[]{:S(2)}, u32[]{:S(2)}) collective-permute-start(bf16[128,8192]{1,0:T(8,128)(2,1)} %collective-permute-done.7), channel_id=1, source_target_pairs={{0,1},{1,2},{2,3},{3,4},{4,5},{5,6},{6,7},{7,8},{8,9},{9,10},{10,1... | collective-permute-start | bytes 6291464 | tf_op jit(solution)/shard_map/ppermute | solution.py:69
  465.3 47.7 %copy-start.28 = (bf16[128,8192]{1,0:T(8,128)(2,1)S(1)}, bf16[128,8192]{1,0:T(8,128)(2,1)}, u32[]{:S(2)}) copy-start(bf16[128,8192]{1,0:T(8,128)(2,1)} %copy-done.27) | copy-start | bytes 6291460
  465.4 58.9 %collective-permute-start.15 = (bf16[128,8192]{1,0:T(8,128)(2,1)}, bf16[128,8192]{1,0:T(8,128)(2,1)S(1)}, u32[]{:S(2)}, u32[]{:S(2)}) collective-permute-start(bf16[128,8192]{1,0:T(8,128)(2,1)} %collective-permute-done.14), channel_id=1, source_target_pairs={{1,0},{2,1},{3,2},{4,3},{5,4},{6,5},{7,6},{8,7},{9,8},{10,9},{11,1... | collective-permute-start | bytes 6291464 | tf_op jit(solution)/shard_map/ppermute | solution.py:72
  511.1 2.2 copy-start.26
  585.2 38.4 %copy-start.39 = (f32[8]{0:T(128)S(1)}, f32[8]{0:T(128)}, u32[]{:S(2)}) copy-start(f32[8]{0:T(128)} %param.30) | copy-start | bytes 100
  585.2 39.0 %copy-start.33 = (f32[512]{0:T(512)S(1)}, f32[512]{0:T(512)}, u32[]{:S(2)}) copy-start(f32[512]{0:T(512)} %param.26) | copy-start | bytes 6148
  610.3 13.8 %collective-permute-start.16 = (bf16[3,512]{1,0:T(4,128)(2,1)S(1)}, bf16[3,512]{1,0:T(4,128)(2,1)S(1)}, u32[]{:S(2)}, u32[]{:S(2)}) collective-permute-start(bf16[3,512]{1,0:T(4,128)(2,1)S(1)} %slice.81), channel_id=1, source_target_pairs={{0,16},{16,32},{32,48},{48,64},{64,80},{80,96},{96,112},{1,17},{17... | collective-permute-start | bytes 9224 | tf_op jit(solution)/shard_map/ppermute | solution.py:22
  624.1 7.8 copy-start.29
  637.3 82.4 %copy-start.37 = (f32[8]{0:T(128)S(1)}, f32[8]{0:T(128)}, u32[]{:S(2)}) copy-start(f32[8]{0:T(128)} %param.29) | copy-start | bytes 100
  759.3 16.4 %collective-permute-start = (f32[8,64,64]{2,1,0:T(8,128)S(1)}, f32[8,64,64]{2,1,0:T(8,128)S(1)}, u32[]{:S(2)}, u32[]{:S(2)}) collective-permute-start(f32[8,64,64]{2,1,0:T(8,128)S(1)} %get-tuple-element.430), channel_id=1, source_target_pairs={{0,16},{16,32},{32,48},{48,64},{64,80},{80,96},{96,112},{1,17},{17... | collective-permute-start | bytes 393224 | tf_op jit(solution)/shard_map/while/body/eval_jaxpr/ppermute | solution.py:22
  776.4 7.7 collective-permute-start
  784.8 7.7 collective-permute-start
  793.1 7.7 collective-permute-start
  801.5 7.7 collective-permute-start
  809.9 7.7 collective-permute-start
  818.3 7.7 collective-permute-start
  (23 other events, 32.8 us)
Sparse Core Ops, SparseCore 0:
  632.1 87.5 all-reduce.2
